TPU v7x, 32 devices: a whole 2x2x4 slice. The times are simulated.
32 devices in a mesh: section: 2 (over core), tensor: 4 (over y, x), expert: 4 (over z).
Axes of the slice: x: 2, y: 2, z: 4, core: 2. Of those that a mesh axis runs over, the one named last changes fastest.
Arguments:
- tokens: bfloat16 [2, 4, 256, 768], P(None, 'expert', 'tensor'), may hold values from -6 to 6
- cotangent: float32 [2, 4, 256, 768], P(None, 'expert', 'tensor'), may hold values from -6 to 6
- norm_gains: float32 [2, 2, 768], P('section'), may hold values from 0.5 to 1.5
- norm_shifts: float32 [2, 2, 768], P('section'), may hold values from -3 to 3
- w_qkv: bfloat16 [2, 3, 768, 12, 64], P('section', None, None, 'tensor'), may hold values from -0.21875 to 0.21875
- w_attn_out: bfloat16 [2, 12, 64, 768], P('section', 'tensor'), may hold values from -0.21875 to 0.21875
- w_router: bfloat16 [2, 768, 8], P('section'), may hold values from -0.21875 to 0.21875
- w_in: bfloat16 [2, 8, 768, 3072], P('section', 'expert', None, 'tensor'), may hold values from -0.21875 to 0.21875
- w_out: bfloat16 [2, 8, 3072, 768], P('section', 'expert', 'tensor'), may hold values from -0.3125 to 0.3125
- choices: int32 [2, 2, 4, 256, 2], P('section', None, 'expert'), may hold values from 0 to 7, as said below
- slot_ranks: int32 [2, 2, 4, 256, 2], P('section', None, 'expert'), may hold values from 0 to 64, as said below
Outputs:
- section_out: bfloat16 [2, 2, 4, 256, 768], P('section', None, 'expert', 'tensor')
- input_grad: bfloat16 [2, 2, 4, 256, 768], P('section', None, 'expert', 'tensor')
- grad_norm_gains: float32 [2, 2, 768], P('section')
- grad_norm_shifts: float32 [2, 2, 768], P('section')
- grad_w_qkv: float32 [2, 3, 768, 12, 64], P('section', None, None, 'tensor')
- grad_w_attn_out: float32 [2, 12, 64, 768], P('section', 'tensor')
- grad_w_router: float32 [2, 768, 8], P('section')
- grad_w_in: float32 [2, 8, 768, 3072], P('section', 'expert', None, 'tensor')
- grad_w_out: float32 [2, 8, 3072, 768], P('section', 'expert', 'tensor')
Inputs may be any that keep to these rules, and one draw needn't show every extreme that they name: `choices`: the two experts of a token differ. slot_ranks[s, m, row, k] counts the earlier entries that name the same expert in the same block of 256 rows (one index of the expert axis, one section, one micro-batch), where all first choices of the block come before all second choices and rows go in order; it is 64 where that count is 64 or more.
All inputs are finite; a program needn't handle non-finite values.
Results may differ from a plain program's by a relative error of at most 0.025.
Values may be sent and summed in bfloat16 or wider, within the bound.
No kernel may reach another device: no remote copies, remote signals or barrier semaphores. Data moves between devices by JAX's collectives and lax.ppermute only.
A program may use at most 128 MiB of HBM per device.

v0:
```python
import jax
import jax.numpy as jnp
from jax import lax
from jax.sharding import PartitionSpec as P

HEAD_DIM = 64
norm_eps = 1e-06
half_root = 0.7071067811865476
tau_root = 0.3989422804014327
highest = lax.Precision.HIGHEST


def shifted(block, axis, distance):
    devices = range(lax.axis_size(axis))
    route = [(i - distance, i) for i in devices if i - distance in devices]
    return lax.ppermute(block, axis, route)


def gelu_value(values):
    return 0.5 * values * (1.0 + lax.erf(values * half_root))


def gelu_slope(values):
    return (
        0.5 * (1.0 + lax.erf(values * half_root))
        + values * jnp.exp(-0.5 * values * values) * tau_root
    )


def normalize(values, gain_row, shift_row):
    center = jnp.mean(values, axis=-1, keepdims=True)
    deviation = values - center
    factor = lax.rsqrt(jnp.mean(deviation * deviation, axis=-1, keepdims=True) + norm_eps)
    unit_rows = deviation * factor
    return (unit_rows * gain_row + shift_row, unit_rows, factor)


def norm_back(grad_norm, unit_rows, factor, gain_row):
    scaled = grad_norm * gain_row
    return factor * (
        scaled
        - jnp.mean(scaled, axis=-1, keepdims=True)
        - unit_rows * jnp.mean(scaled * unit_rows, axis=-1, keepdims=True)
    )


def gather_rows(block_part):
    return lax.all_gather(block_part, "tensor", axis=1, tiled=True)


def sum_rows(block_terms):
    return lax.psum_scatter(
        block_terms.astype(jnp.bfloat16), "tensor", scatter_dimension=1, tiled=True
    ).astype(jnp.float32)


def forward(block_rows, weights_all, expert_picks, slot_picks):
    gain_rows, shift_rows, w_qkv, w_attn, w_router, w_first, w_second = weights_all
    images = expert_picks.shape[0]
    length = expert_picks.shape[1]
    feature_count = block_rows.shape[2]
    experts = w_router.shape[1]
    capacity = 2 * images * length // experts
    dump_cell = experts * capacity
    owner_count = lax.axis_size("expert")
    local_count = experts // owner_count
    score_scale = HEAD_DIM ** (-0.5)
    head_count = w_qkv.shape[2] // HEAD_DIM
    start_rows = block_rows.astype(jnp.float32)
    normed_one, unit_one, factor_one = normalize(start_rows, gain_rows[0], shift_rows[0])
    full_one = gather_rows(normed_one.astype(jnp.bfloat16))
    qkv_rows = jnp.einsum(
        "isd,kdh->kish", full_one, w_qkv, preferred_element_type=jnp.float32
    ).astype(jnp.bfloat16)
    qkv_heads = qkv_rows.reshape(3, images, length, head_count, HEAD_DIM)
    scores = (
        jnp.einsum(
            "ishd,ithd->ihst", qkv_heads[0], qkv_heads[1], preferred_element_type=jnp.float32
        )
        * score_scale
    )
    log_total = jnp.log(jnp.sum(jnp.exp(scores), axis=-1, keepdims=True))
    weights_soft = jnp.exp(scores - log_total).astype(jnp.bfloat16)
    attended = (
        jnp.einsum(
            "ihst,ithd->ishd", weights_soft, qkv_heads[2], preferred_element_type=jnp.float32
        )
        .astype(jnp.bfloat16)
        .reshape(images, length, -1)
    )
    middle = start_rows + sum_rows(
        jnp.einsum("ish,hd->isd", attended, w_attn, preferred_element_type=jnp.float32)
    )
    normed_two, unit_two, factor_two = normalize(middle, gain_rows[1], shift_rows[1])
    own_two = normed_two.astype(jnp.bfloat16)
    full_two = gather_rows(own_two)
    logits = jnp.einsum("isd,de->ise", full_two, w_router, preferred_element_type=jnp.float32)
    pick_table = (expert_picks[..., None] == jnp.arange(experts)).astype(jnp.float32)
    chosen = jnp.sum(pick_table * logits[:, :, None, :], axis=-1)
    first_gate = jax.nn.sigmoid(chosen[..., 0] - chosen[..., 1])
    gate_pair = jnp.stack([first_gate, 1.0 - first_gate], axis=-1)
    cell_index = jnp.where(slot_picks < capacity, expert_picks * capacity + slot_picks, dump_cell)
    copies = jnp.broadcast_to(full_two[:, :, None, :], (images, length, 2, feature_count)).reshape(
        -1, feature_count
    )
    sending = (
        jnp.zeros((dump_cell + 1, feature_count), jnp.bfloat16)
        .at[cell_index.reshape(-1)]
        .set(copies)
    )
    sending = sending[:dump_cell].reshape(owner_count, local_count, capacity, feature_count)
    arrived = lax.all_to_all(sending, "expert", split_axis=0, concat_axis=0, tiled=True)
    inner_rows = jnp.einsum("sjcd,jdf->sjcf", arrived, w_first, preferred_element_type=jnp.float32)
    hidden = gelu_value(inner_rows).astype(jnp.bfloat16)
    partial_out = jnp.einsum("sjcf,jfd->sjcd", hidden, w_second, preferred_element_type=jnp.float32)
    zero_row = jnp.zeros((1, feature_count), jnp.float32)
    returned = lax.all_to_all(
        partial_out.astype(jnp.bfloat16), "expert", split_axis=0, concat_axis=0, tiled=True
    ).astype(partial_out.dtype)
    table_out = jnp.concatenate([returned.reshape(dump_cell, feature_count), zero_row], axis=0)
    mixed_rows = sum_rows(jnp.sum(gate_pair[..., None] * table_out[cell_index], axis=2))
    result = (middle + mixed_rows).astype(jnp.bfloat16)
    kept_state = (
        unit_one,
        factor_one,
        full_one,
        qkv_rows,
        log_total,
        attended,
        unit_two,
        factor_two,
        own_two,
        full_two,
        pick_table,
        gate_pair,
        cell_index,
        arrived,
        inner_rows,
        hidden,
        table_out,
    )
    return (result, kept_state)


def backward(grad_rows, weights_all, expert_picks, kept_state):
    gain_rows, shift_rows, w_qkv, w_attn, w_router, w_first, w_second = weights_all
    (
        unit_one,
        factor_one,
        full_one,
        qkv_rows,
        log_total,
        attended,
        unit_two,
        factor_two,
        own_two,
        full_two,
        pick_table,
        gate_pair,
        cell_index,
        arrived,
        inner_rows,
        hidden,
        table_out,
    ) = kept_state
    images = expert_picks.shape[0]
    length = expert_picks.shape[1]
    feature_count = grad_rows.shape[2]
    experts = w_router.shape[1]
    capacity = 2 * images * length // experts
    dump_cell = experts * capacity
    owner_count = lax.axis_size("expert")
    local_count = experts // owner_count
    score_scale = HEAD_DIM ** (-0.5)
    head_count = w_qkv.shape[2] // HEAD_DIM
    full_grad = gather_rows(grad_rows.astype(jnp.bfloat16))
    full_wide = full_grad.astype(jnp.float32)
    pieces = (
        (gate_pair[..., None] * full_wide[:, :, None, :])
        .astype(jnp.bfloat16)
        .reshape(-1, feature_count)
    )
    back_send = (
        jnp.zeros((dump_cell + 1, feature_count), jnp.bfloat16)
        .at[cell_index.reshape(-1)]
        .set(pieces)
    )
    back_send = back_send[:dump_cell].reshape(owner_count, local_count, capacity, feature_count)
    back_arrived = lax.all_to_all(back_send, "expert", split_axis=0, concat_axis=0, tiled=True)
    hidden_grad = jnp.einsum(
        "sjcd,jfd->sjcf", back_arrived, w_second, preferred_element_type=jnp.float32
    )
    inner_grad = (hidden_grad * gelu_slope(inner_rows)).astype(jnp.bfloat16)
    grad_second = jnp.einsum(
        "sjcf,sjcd->jfd", hidden, back_arrived, preferred_element_type=jnp.float32
    )
    grad_first = jnp.einsum(
        "sjcd,sjcf->jdf", arrived, inner_grad, preferred_element_type=jnp.float32
    )
    input_part = jnp.einsum(
        "sjcf,jdf->sjcd", inner_grad, w_first, preferred_element_type=jnp.float32
    )
    zero_row = jnp.zeros((1, feature_count), jnp.float32)
    sign_table = pick_table[:, :, 0, :] - pick_table[:, :, 1, :]
    input_back = lax.all_to_all(
        input_part.astype(jnp.bfloat16), "expert", split_axis=0, concat_axis=0, tiled=True
    ).astype(input_part.dtype)
    table_in = jnp.concatenate([input_back.reshape(dump_cell, feature_count), zero_row], axis=0)
    routed = jnp.sum(table_in[cell_index], axis=2)
    gate_grad = jnp.sum(full_wide[:, :, None, :] * table_out[cell_index], axis=-1)
    logit_grad = (gate_pair[..., 0] * gate_pair[..., 1] * (gate_grad[..., 0] - gate_grad[..., 1]))[
        ..., None
    ] * sign_table
    grad_router = jnp.einsum(
        "isd,ise->de", full_two, logit_grad, precision=highest, preferred_element_type=jnp.float32
    )
    normed_grad = sum_rows(
        routed
        + jnp.einsum(
            "ise,de->isd",
            logit_grad,
            w_router,
            precision=highest,
            preferred_element_type=jnp.float32,
        )
    )
    mid_grad = grad_rows + norm_back(normed_grad, unit_two, factor_two, gain_rows[1])
    gain_two = jnp.sum(normed_grad * unit_two, axis=(0, 1))
    shift_two = jnp.sum(normed_grad, axis=(0, 1))
    full_mid = gather_rows(mid_grad.astype(jnp.bfloat16))
    grad_attn = jnp.einsum("ish,isd->hd", attended, full_mid, preferred_element_type=jnp.float32)
    attended_grad = (
        jnp.einsum("isd,hd->ish", full_mid, w_attn, preferred_element_type=jnp.float32)
        .astype(jnp.bfloat16)
        .reshape(images, length, head_count, HEAD_DIM)
    )
    qkv_heads = qkv_rows.reshape(3, images, length, head_count, HEAD_DIM)
    scores = (
        jnp.einsum(
            "ishd,ithd->ihst", qkv_heads[0], qkv_heads[1], preferred_element_type=jnp.float32
        )
        * score_scale
    )
    probs_wide = jnp.exp(scores - log_total)
    value_grad = jnp.einsum(
        "ihst,ishd->ithd",
        probs_wide.astype(jnp.bfloat16),
        attended_grad,
        preferred_element_type=jnp.float32,
    ).astype(jnp.bfloat16)
    prob_grad = jnp.einsum(
        "ishd,ithd->ihst", attended_grad, qkv_heads[2], preferred_element_type=jnp.float32
    )
    row_dot = jnp.sum(probs_wide * prob_grad, axis=-1, keepdims=True)
    score_grad = (probs_wide * (prob_grad - row_dot) * score_scale).astype(jnp.bfloat16)
    query_grad = jnp.einsum(
        "ihst,ithd->ishd", score_grad, qkv_heads[1], preferred_element_type=jnp.float32
    ).astype(jnp.bfloat16)
    key_grad = jnp.einsum(
        "ihst,ishd->ithd", score_grad, qkv_heads[0], preferred_element_type=jnp.float32
    ).astype(jnp.bfloat16)
    qkv_grad = jnp.stack([query_grad, key_grad, value_grad]).reshape(3, images, length, -1)
    grad_qkv = jnp.einsum("isd,kish->kdh", full_one, qkv_grad, preferred_element_type=jnp.float32)
    first_grad = sum_rows(
        jnp.einsum("kish,kdh->isd", qkv_grad, w_qkv, preferred_element_type=jnp.float32)
    )
    start_grad = mid_grad + norm_back(first_grad, unit_one, factor_one, gain_rows[0])
    gain_one = jnp.sum(first_grad * unit_one, axis=(0, 1))
    shift_one = jnp.sum(first_grad, axis=(0, 1))
    grad_parts = (
        jnp.stack([gain_one, gain_two]),
        jnp.stack([shift_one, shift_two]),
        grad_qkv,
        grad_attn,
        grad_router,
        grad_first,
        grad_second,
    )
    return (start_grad.astype(jnp.bfloat16), grad_parts)


def per_device(
    tokens,
    cotangent,
    norm_gains,
    norm_shifts,
    w_qkv,
    w_attn_out,
    w_router,
    w_in,
    w_out,
    choices,
    slot_ranks,
):
    section_index = lax.axis_index("section")
    micro_count = tokens.shape[0]
    feature_count = tokens.shape[3]
    weights_all = (
        norm_gains[0],
        norm_shifts[0],
        w_qkv[0].reshape(3, feature_count, -1),
        w_attn_out[0].reshape(-1, feature_count),
        w_router[0],
        w_in[0],
        w_out[0],
    )
    received = jnp.zeros(tokens.shape[1:], jnp.bfloat16)
    produced = []
    kept_list = []
    for moment in range(micro_count + 1):
        if moment < micro_count:
            fresh_rows = tokens[moment]
        else:
            fresh_rows = jnp.zeros(tokens.shape[1:], jnp.bfloat16)
        block_rows = jnp.where(section_index == 0, fresh_rows, received)
        micro_index = jnp.clip(moment - section_index, 0, micro_count - 1)
        expert_picks = lax.dynamic_index_in_dim(choices[0], micro_index, 0, keepdims=False)
        slot_picks = lax.dynamic_index_in_dim(slot_ranks[0], micro_index, 0, keepdims=False)
        result, kept_state = forward(block_rows, weights_all, expert_picks, slot_picks)
        received = shifted(result, "section", 1)
        produced.append(result)
        kept_list.append((kept_state, expert_picks))
    section_out = lax.dynamic_slice_in_dim(jnp.stack(produced), section_index, micro_count, 0)[None]
    returned_grad = jnp.zeros(cotangent.shape[1:], jnp.float32)
    input_grads = []
    totals = None
    for moment in range(micro_count + 1):
        micro_late = micro_count - 1 - moment
        if micro_late >= 0:
            outer_grad = cotangent[micro_late]
        else:
            outer_grad = jnp.zeros(cotangent.shape[1:], jnp.float32)
        grad_rows = jnp.where(section_index == 1, outer_grad, returned_grad)
        kept_state, expert_picks = kept_list[micro_count - moment]
        grad_input, grad_parts = backward(grad_rows, weights_all, expert_picks, kept_state)
        returned_grad = shifted(grad_input, "section", -1).astype(jnp.float32)
        input_grads.append(grad_input)
        totals = grad_parts if totals is None else jax.tree.map(jnp.add, totals, grad_parts)
    input_grad = lax.dynamic_slice_in_dim(
        jnp.stack(input_grads[::-1]), section_index, micro_count, 0
    )[None]
    gain_sum, shift_sum, qkv_sum, attn_sum, router_sum, first_sum, second_sum = totals
    qkv_total, attn_total = (
        lax.psum(qkv_sum.astype(jnp.bfloat16), "expert").astype(jnp.float32),
        lax.psum(attn_sum.astype(jnp.bfloat16), "expert").astype(jnp.float32),
    )
    gain_total, shift_total, router_total = lax.psum(
        (gain_sum, shift_sum, router_sum), ("tensor", "expert")
    )
    return (
        section_out,
        input_grad,
        gain_total[None],
        shift_total[None],
        qkv_total.reshape(w_qkv.shape),
        attn_total.reshape(w_attn_out.shape),
        router_total[None],
        first_sum[None],
        second_sum[None],
    )


def solution(mesh):
    return jax.shard_map(
        per_device,
        mesh=mesh,
        in_specs=(
            P(None, "expert", "tensor", None),
            P(None, "expert", "tensor", None),
            P("section", None, None),
            P("section", None, None),
            P("section", None, None, "tensor", None),
            P("section", "tensor", None, None),
            P("section", None, None),
            P("section", "expert", None, "tensor"),
            P("section", "expert", "tensor", None),
            P("section", None, "expert", None, None),
            P("section", None, "expert", None, None),
        ),
        out_specs=(
            P("section", None, "expert", "tensor", None),
            P("section", None, "expert", "tensor", None),
            P("section", None, None),
            P("section", None, None),
            P("section", None, None, "tensor", None),
            P("section", "tensor", None, None),
            P("section", None, None),
            P("section", "expert", None, "tensor"),
            P("section", "expert", "tensor", None),
        ),
        check_vma=False,
    )
```

profile of v0, /device:TPU:0, one launch (start us, length us, event | category | flops | bytes accessed | tf_op | source)
XLA Modules:
  0.0 1035.5 jit_solution(583829729808899617)
XLA Ops:
  11.4 11.0 %all_gather.36 = bf16[1,256,768]{2,1,0:T(8,128)(2,1)S(1)} all-gather(bf16[1,64,768]{2,1,0:T(8,128)(2,1)S(1)} %fusion.265), channel_id=1, replica_groups=mesh['section'=2,'tensor'=4,'expert'=4] {'tensor'}, dimensions={1}, use_global_device_ids=true | all-gather | bytes 491520 | tf_op jit(solution)/shard_map/all_gather | solution.py:48
  29.3 24.2 %reduce-scatter.13.cloned.1.call-done = bf16[1,64,768]{2,1,0:T(8,128)(2,1)} async-done(((bf16[1,256,768]{2,1,0:T(8,128)(2,1)}), bf16[1,64,768]{2,1,0:T(8,128)(2,1)}) %reduce-scatter.13.cloned.1.call-update) | async-done | bytes 98320 | tf_op jit(solution)/shard_map/reduce_scatter | solution.py:52
  56.7 9.9 all_gather.37
  76.3 21.7 %all_to_all.60 = bf16[4,2,64,768]{3,2,1,0:T(8,128)(2,1)S(1)} all-to-all(bf16[4,2,64,768]{3,2,1,0:T(8,128)(2,1)S(1)} %bitcast.669), channel_id=1, replica_groups=mesh['section'=2,'tensor'=4,'expert'=4] {'expert'}, dimensions={0} | all-to-all | bytes 1572864 | tf_op jit(solution)/shard_map/all_to_all | solution.py:112
  101.1 4.2 all-to-all-start.1
  107.6 16.3 %all-to-all-done.1 = bf16[4,2,64,768]{3,2,1,0:T(8,128)(2,1)} async-done(((bf16[4,2,64,768]{3,2,1,0:T(8,128)(2,1)}), bf16[4,2,64,768]{3,2,1,0:T(8,128)(2,1)}, u32[]{:S(2)}, u32[]{:S(2)}) %all-to-all-start.1) | async-done | bytes 786464 | tf_op jit(solution)/shard_map/all_to_all | solution.py:117
  126.2 4.6 gather_fusion
  138.1 22.9 %reduce-scatter.15.cloned.1.call-done = bf16[1,64,768]{2,1,0:T(8,128)(2,1)} async-done(((bf16[1,256,768]{2,1,0:T(8,128)(2,1)}), bf16[1,64,768]{2,1,0:T(8,128)(2,1)}) %reduce-scatter.15.cloned.1.call-update) | async-done | bytes 98320 | tf_op jit(solution)/shard_map/reduce_scatter | solution.py:52
  164.7 9.5 all_gather.38
  184.1 22.5 %reduce-scatter.17.cloned.1.call-done = bf16[1,64,768]{2,1,0:T(8,128)(2,1)} async-done(((bf16[1,256,768]{2,1,0:T(8,128)(2,1)}), bf16[1,64,768]{2,1,0:T(8,128)(2,1)}) %reduce-scatter.17.cloned.1.call-update) | async-done | bytes 98320 | tf_op jit(solution)/shard_map/reduce_scatter | solution.py:52
  209.8 9.9 all_gather.39
  229.4 22.2 %all_to_all.61 = bf16[4,2,64,768]{3,2,1,0:T(8,128)(2,1)S(1)} all-to-all(bf16[4,2,64,768]{3,2,1,0:T(8,128)(2,1)S(1)} %bitcast.670), channel_id=1, replica_groups=mesh['section'=2,'tensor'=4,'expert'=4] {'expert'}, dimensions={0} | all-to-all | bytes 1572864 | tf_op jit(solution)/shard_map/all_to_all | solution.py:112
  254.6 4.2 all-to-all-start.3
  260.2 17.1 %all-to-all-done.3 = bf16[4,2,64,768]{3,2,1,0:T(8,128)(2,1)} async-done(((bf16[4,2,64,768]{3,2,1,0:T(8,128)(2,1)}), bf16[4,2,64,768]{3,2,1,0:T(8,128)(2,1)}, u32[]{:S(2)}, u32[]{:S(2)}) %all-to-all-start.3) | async-done | bytes 786464 | tf_op jit(solution)/shard_map/all_to_all | solution.py:117
  279.7 4.6 gather_fusion.1
  287.3 4.2 multiply_reduce_fusion.4
  291.6 22.9 %reduce-scatter.19.cloned.1.call-done = bf16[1,64,768]{2,1,0:T(8,128)(2,1)} async-done(((bf16[1,256,768]{2,1,0:T(8,128)(2,1)}), bf16[1,64,768]{2,1,0:T(8,128)(2,1)}) %reduce-scatter.19.cloned.1.call-update) | async-done | bytes 98320 | tf_op jit(solution)/shard_map/reduce_scatter | solution.py:52
  318.2 9.5 all_gather.40
  332.9 24.6 %reduce-scatter.21.cloned.1.call-done = bf16[1,64,768]{2,1,0:T(8,128)(2,1)} async-done(((bf16[1,256,768]{2,1,0:T(8,128)(2,1)}), bf16[1,64,768]{2,1,0:T(8,128)(2,1)}) %reduce-scatter.21.cloned.1.call-update) | async-done | bytes 98320 | tf_op jit(solution)/shard_map/reduce_scatter | solution.py:52
  360.7 10.1 all_gather.41
  381.2 4.6 all-to-all-start.4
  386.8 8.1 all_gather.42
  401.3 4.5 scatter_custom_fusion.3
  408.0 5.1 all-to-all-start.6
  416.9 12.5 %all-to-all-done.6 = bf16[4,2,64,768]{3,2,1,0:T(8,128)(2,1)} async-done(((bf16[4,2,64,768]{3,2,1,0:T(8,128)(2,1)}), bf16[4,2,64,768]{3,2,1,0:T(8,128)(2,1)}, u32[]{:S(2)}, u32[]{:S(2)}) %all-to-all-start.6) | async-done | bytes 786464 | tf_op jit(solution)/shard_map/all_to_all | solution.py:189
  434.0 4.4 all-to-all-start.7
  441.6 13.4 %all-to-all-done.7 = bf16[4,2,64,768]{3,2,1,0:T(8,128)(2,1)} async-done(((bf16[4,2,64,768]{3,2,1,0:T(8,128)(2,1)}), bf16[4,2,64,768]{3,2,1,0:T(8,128)(2,1)}, u32[]{:S(2)}, u32[]{:S(2)}) %all-to-all-start.7) | async-done | bytes 786464 | tf_op jit(solution)/shard_map/all_to_all | solution.py:205
  455.0 4.2 all-to-all-start.5
  462.1 4.6 gather_fusion.3
  469.8 7.0 all-to-all-done.5
  479.1 4.6 gather_fusion.2
  486.8 5.0 multiply_reduce_fusion.2
  491.8 4.2 reduce.49
  501.8 20.1 %reduce-scatter.25.cloned.1.call-done = bf16[1,64,768]{2,1,0:T(8,128)(2,1)} async-done(((bf16[1,256,768]{2,1,0:T(8,128)(2,1)}), bf16[1,64,768]{2,1,0:T(8,128)(2,1)}) %reduce-scatter.25.cloned.1.call-update) | async-done | bytes 98320 | tf_op jit(solution)/shard_map/reduce_scatter | solution.py:52
  524.0 26.0 %reduce-scatter.23.cloned.1.call-done = bf16[1,64,768]{2,1,0:T(8,128)(2,1)} async-done(((bf16[1,256,768]{2,1,0:T(8,128)(2,1)}), bf16[1,64,768]{2,1,0:T(8,128)(2,1)}) %reduce-scatter.23.cloned.1.call-update) | async-done | bytes 98320 | tf_op jit(solution)/shard_map/reduce_scatter | solution.py:52
  551.6 10.3 all_gather.43
  576.6 24.9 %reduce-scatter.27.cloned.1.call-done = bf16[1,64,768]{2,1,0:T(8,128)(2,1)} async-done(((bf16[1,256,768]{2,1,0:T(8,128)(2,1)}), bf16[1,64,768]{2,1,0:T(8,128)(2,1)}) %reduce-scatter.27.cloned.1.call-update) | async-done | bytes 98320 | tf_op jit(solution)/shard_map/reduce_scatter | solution.py:52
  608.8 9.5 all_gather.44
  623.1 4.5 scatter_custom_fusion.4
  628.7 22.8 %all_to_all.62 = bf16[4,2,64,768]{3,2,1,0:T(8,128)(2,1)S(1)} all-to-all(bf16[4,2,64,768]{3,2,1,0:T(8,128)(2,1)S(1)} %bitcast.665), channel_id=1, replica_groups=mesh['section'=2,'tensor'=4,'expert'=4] {'expert'}, dimensions={0} | all-to-all | bytes 1572864 | tf_op jit(solution)/shard_map/all_to_all | solution.py:189
  655.3 4.2 all-to-all-start.9
  665.6 12.9 %all-to-all-done.9 = bf16[4,2,64,768]{3,2,1,0:T(8,128)(2,1)} async-done(((bf16[4,2,64,768]{3,2,1,0:T(8,128)(2,1)}), bf16[4,2,64,768]{3,2,1,0:T(8,128)(2,1)}, u32[]{:S(2)}, u32[]{:S(2)}) %all-to-all-start.9) | async-done | bytes 786464 | tf_op jit(solution)/shard_map/all_to_all | solution.py:205
  681.0 4.6 gather_fusion.4
  688.6 4.2 reduce.50
  698.0 20.4 %reduce-scatter.29.cloned.1.call-done = bf16[1,64,768]{2,1,0:T(8,128)(2,1)} async-done(((bf16[1,256,768]{2,1,0:T(8,128)(2,1)}), bf16[1,64,768]{2,1,0:T(8,128)(2,1)}) %reduce-scatter.29.cloned.1.call-update) | async-done | bytes 98320 | tf_op jit(solution)/shard_map/reduce_scatter | solution.py:52
  721.7 9.9 all_gather.45
  745.8 23.7 %reduce-scatter.31.cloned.1.call-done = bf16[1,64,768]{2,1,0:T(8,128)(2,1)} async-done(((bf16[1,256,768]{2,1,0:T(8,128)(2,1)}), bf16[1,64,768]{2,1,0:T(8,128)(2,1)}) %reduce-scatter.31.cloned.1.call-update) | async-done | bytes 98320 | tf_op jit(solution)/shard_map/reduce_scatter | solution.py:52
  775.9 10.5 %all_gather.46 = bf16[1,256,768]{2,1,0:T(8,128)(2,1)S(1)} all-gather(bf16[1,64,768]{2,1,0:T(8,128)(2,1)S(1)} %fusion.298), channel_id=1, replica_groups=mesh['section'=2,'tensor'=4,'expert'=4] {'tensor'}, dimensions={1}, use_global_device_ids=true | all-gather | bytes 491520 | tf_op jit(solution)/shard_map/all_gather | solution.py:48
  791.3 4.5 scatter_custom_fusion.5
  797.8 4.6 all-to-all-start.10
  802.4 4.4 fusion.163
  806.9 4.2 fusion.179
  816.0 6.4 all-to-all-done.10
  827.0 4.2 all-to-all-start.11
  836.4 4.7 fusion.176
  843.7 7.2 all-to-all-done.11
  853.3 4.6 gather_fusion.5
  866.4 4.5 fusion.161
  877.0 12.3 %reduce-scatter.33.cloned.1.call-done = bf16[1,64,768]{2,1,0:T(8,128)(2,1)} async-done(((bf16[1,256,768]{2,1,0:T(8,128)(2,1)}), bf16[1,64,768]{2,1,0:T(8,128)(2,1)}) %reduce-scatter.33.cloned.1.call-update) | async-done | bytes 98320 | tf_op jit(solution)/shard_map/reduce_scatter | solution.py:52
  891.5 9.9 all_gather.47
  915.4 7.7 fusion.6
  926.6 7.1 fusion.7
  933.7 6.2 reduce-scatter.35.cloned.1.call-done
  942.5 79.7 %all-reduce.6 = (f32[1,2,768]{2,1,0:T(2,128)}, f32[1,2,768]{2,1,0:T(2,128)}, f32[1,768,8]{1,2,0:T(8,128)}) all-reduce(f32[1,2,768]{2,1,0:T(2,128)S(1)} %fusion.357, f32[1,2,768]{2,1,0:T(2,128)S(1)} %fusion.359, f32[1,768,8]{1,2,0:T(8,128)} %fusion.144), channel_id=1, replica_groups=mesh['section'=2,'tensor'=4,'expert'=4] {'tensor','expert'}, use_global_device_ids=true, to_apply=%region_66.67 | all-reduce | flops 9216 | bytes 73728 | tf_op jit(solution)/shard_map/psum | solution.py:347
  (578 shorter events, 280.3 us)
Async XLA Ops:
  7.2 91.9 %copy-start = (bf16[1,2,768,768]{3,2,1,0:T(8,128)(2,1)S(1)}, bf16[1,2,768,768]{3,2,1,0:T(8,128)(2,1)}, u32[]{:S(2)}) copy-start(bf16[1,2,768,768]{3,2,1,0:T(8,128)(2,1)} %param.19) | copy-start | bytes 7077892
  7.2 46.3 %reduce-scatter.13.cloned.1.call-start = ((), (), s32[]{:S(2)}) async-start(), calls=%async_computation.24 | async-start | bytes 491520 | tf_op jit(solution)/shard_map/reduce_scatter | solution.py:52
  10.4 45.3 %copy-start.95 = (f32[768]{0:T(1024)}, f32[768]{0:T(1024)S(1)}, u32[]{:S(2)}) copy-start(f32[768]{0:T(1024)S(1)} %get-tuple-element.38) | copy-start | bytes 9220
  10.4 154.2 %copy-start.59 = (f32[768]{0:T(1024)}, f32[768]{0:T(1024)S(1)}, u32[]{:S(2)}) copy-start(f32[768]{0:T(1024)S(1)} %get-tuple-element.86) | copy-start | bytes 9220
  10.4 154.2 %copy-start.100 = (f32[768]{0:T(1024)}, f32[768]{0:T(1024)S(1)}, u32[]{:S(2)}) copy-start(f32[768]{0:T(1024)S(1)} %get-tuple-element.37) | copy-start | bytes 9220
  24.3 29.2 %copy-start.12 = (bf16[2,1,64,768]{3,2,1,0:T(8,128)(2,1)S(1)}, bf16[2,1,64,768]{3,2,1,0:T(8,128)(2,1)}, u32[]{:S(2)}) copy-start(bf16[2,1,64,768]{3,2,1,0:T(8,128)(2,1)} %param.11) | copy-start | bytes 589828
  27.3 40.6 %copy-start.71 = (bf16[3,64,256]{2,1,0:T(8,128)(2,1)}, bf16[3,64,256]{2,1,0:T(8,128)(2,1)S(1)}, u32[]{:S(2)}) copy-start(bf16[3,64,256]{2,1,0:T(8,128)(2,1)S(1)} %convolution_convert_fusion.14) | copy-start | bytes 294916
  29.3 41.6 %copy-start.149 = (s32[512,1]{0,1:T(1,128)}, s32[512,1]{0,1:T(1,128)S(1)}, u32[]{:S(2)}) copy-start(s32[512,1]{0,1:T(1,128)S(1)} %compare_select_fusion.2) | copy-start | bytes 6148
  66.6 39.9 %copy-start.17 = (bf16[1,256,768]{2,1,0:T(8,128)(2,1)}, bf16[1,256,768]{2,1,0:T(8,128)(2,1)S(1)}, u32[]{:S(2)}) copy-start(bf16[1,256,768]{2,1,0:T(8,128)(2,1)S(1)} %all_gather.37) | copy-start | bytes 1179652
  101.1 22.7 %all-to-all-start.1 = ((bf16[4,2,64,768]{3,2,1,0:T(8,128)(2,1)}), bf16[4,2,64,768]{3,2,1,0:T(8,128)(2,1)}, u32[]{:S(2)}, u32[]{:S(2)}) async-start(bf16[4,2,64,768]{3,2,1,0:T(8,128)(2,1)} %copy.213), calls=%async_computation.2 | async-start | bytes 1572864 | tf_op jit(solution)/shard_map/all_to_all | solution.py:117
  105.3 55.7 %reduce-scatter.15.cloned.1.call-start = ((), (), s32[]{:S(2)}) async-start(), calls=%async_computation.25 | async-start | bytes 491520 | tf_op jit(solution)/shard_map/reduce_scatter | solution.py:52
  106.5 24.3 %copy-start.105 = (s32[256,2]{0,1:T(2,128)}, s32[256,2]{0,1:T(2,128)S(1)}, u32[]{:S(2)}) copy-start(s32[256,2]{0,1:T(2,128)S(1)} %get-tuple-element.77) | copy-start | bytes 6148
  133.8 27.2 %copy-start.23 = (bf16[1,64,768]{2,1,0:T(8,128)(2,1)S(1)}, bf16[1,64,768]{2,1,0:T(8,128)(2,1)}, u32[]{:S(2)}) copy-start(bf16[1,64,768]{2,1,0:T(8,128)(2,1)} %reduce-scatter.13.cloned.1.call-done) | copy-start | bytes 294916
  138.0 68.6 %reduce-scatter.17.cloned.1.call-start = ((), (), s32[]{:S(2)}) async-start(), calls=%async_computation.26 | async-start | bytes 491520 | tf_op jit(solution)/shard_map/reduce_scatter | solution.py:52
  162.0 2.2 collective-permute-start
  177.6 31.1 %copy-start.41 = (f32[3,256,256]{1,2,0:T(8,128)}, f32[3,256,256]{1,2,0:T(8,128)S(1)}, u32[]{:S(2)}) copy-start(f32[3,256,256]{1,2,0:T(8,128)S(1)} %convolution_multiply_fusion.1) | copy-start | bytes 2359300
  177.6 31.1 %copy-start.96 = (f32[768]{0:T(1024)S(1)}, f32[768]{0:T(1024)}, u32[]{:S(2)}) copy-start(f32[768]{0:T(1024)} %copy-done.95) | copy-start | bytes 9220
  219.7 39.5 %copy-start.19 = (bf16[1,256,768]{2,1,0:T(8,128)(2,1)}, bf16[1,256,768]{2,1,0:T(8,128)(2,1)S(1)}, u32[]{:S(2)}) copy-start(bf16[1,256,768]{2,1,0:T(8,128)(2,1)S(1)} %all_gather.39) | copy-start | bytes 1179652
  254.6 22.7 %all-to-all-start.3 = ((bf16[4,2,64,768]{3,2,1,0:T(8,128)(2,1)}), bf16[4,2,64,768]{3,2,1,0:T(8,128)(2,1)}, u32[]{:S(2)}, u32[]{:S(2)}) async-start(bf16[4,2,64,768]{3,2,1,0:T(8,128)(2,1)} %copy.219), calls=%async_computation.6 | async-start | bytes 1572864 | tf_op jit(solution)/shard_map/all_to_all | solution.py:117
  258.8 55.7 %reduce-scatter.19.cloned.1.call-start = ((), (), s32[]{:S(2)}) async-start(), calls=%async_computation.27 | async-start | bytes 491520 | tf_op jit(solution)/shard_map/reduce_scatter | solution.py:52
  259.5 24.8 %copy-start.121 = (f32[1,256,1]{1,2,0:T(1,128)}, f32[1,256,1]{1,2,0:T(1,128)S(1)}, u32[]{:S(2)}) copy-start(f32[1,256,1]{1,2,0:T(1,128)S(1)} %get-tuple-element.53) | copy-start | bytes 3076
  287.3 27.2 %copy-start.33 = (bf16[1,64,768]{2,1,0:T(8,128)(2,1)S(1)}, bf16[1,64,768]{2,1,0:T(8,128)(2,1)}, u32[]{:S(2)}) copy-start(bf16[1,64,768]{2,1,0:T(8,128)(2,1)} %reduce-scatter.17.cloned.1.call-done) | copy-start | bytes 294916
  287.3 30.8 %copy-start.60 = (f32[768]{0:T(1024)S(1)}, f32[768]{0:T(1024)}, u32[]{:S(2)}) copy-start(f32[768]{0:T(1024)} %copy-done.59) | copy-start | bytes 9220
  287.3 30.8 %copy-start.101 = (f32[768]{0:T(1024)S(1)}, f32[768]{0:T(1024)}, u32[]{:S(2)}) copy-start(f32[768]{0:T(1024)} %copy-done.100) | copy-start | bytes 9220
  291.5 66.0 %reduce-scatter.21.cloned.1.call-start = ((), (), s32[]{:S(2)}) async-start(), calls=%async_computation.28 | async-start | bytes 491520 | tf_op jit(solution)/shard_map/reduce_scatter | solution.py:52
  315.6 2.2 collective-permute-start.1
  329.7 29.9 %copy-start.97 = (f32[768]{0:T(1024)S(1)}, f32[768]{0:T(1024)}, u32[]{:S(2)}) copy-start(f32[768]{0:T(1024)} %copy-done.95) | copy-start | bytes 9220
  331.5 40.6 %copy-start.64 = (bf16[3,64,256]{2,1,0:T(8,128)(2,1)}, bf16[3,64,256]{2,1,0:T(8,128)(2,1)S(1)}, u32[]{:S(2)}) copy-start(bf16[3,64,256]{2,1,0:T(8,128)(2,1)S(1)} %convolution_convert_fusion.12) | copy-start | bytes 294916
  358.6 163.3 %copy-start.132 = (f32[64]{0:T(128)}, f32[64]{0:T(128)S(1)}, u32[]{:S(2)}) copy-start(f32[64]{0:T(128)S(1)} %broadcast_multiply_fusion.12) | copy-start | bytes 772
  359.7 162.2 %copy-start.147 = (f32[64]{0:T(128)}, f32[64]{0:T(128)S(1)}, u32[]{:S(2)}) copy-start(f32[64]{0:T(128)S(1)} %add_rsqrt_fusion) | copy-start | bytes 772
  370.8 29.9 %copy-start.20 = (bf16[1,256,768]{2,1,0:T(8,128)(2,1)}, bf16[1,256,768]{2,1,0:T(8,128)(2,1)S(1)}, u32[]{:S(2)}) copy-start(bf16[1,256,768]{2,1,0:T(8,128)(2,1)S(1)} %all_gather.41) | copy-start | bytes 1179652
  381.2 26.7 %all-to-all-start.4 = ((bf16[4,2,64,768]{3,2,1,0:T(8,128)(2,1)}), bf16[4,2,64,768]{3,2,1,0:T(8,128)(2,1)}, u32[]{:S(2)}, u32[]{:S(2)}) async-start(bf16[4,2,64,768]{3,2,1,0:T(8,128)(2,1)} %bitcast.666), calls=%async_computation.9 | async-start | bytes 1572864 | tf_op jit(solution)/shard_map/all_to_all | solution.py:112
  408.0 21.4 %all-to-all-start.6 = ((bf16[4,2,64,768]{3,2,1,0:T(8,128)(2,1)}), bf16[4,2,64,768]{3,2,1,0:T(8,128)(2,1)}, u32[]{:S(2)}, u32[]{:S(2)}) async-start(bf16[4,2,64,768]{3,2,1,0:T(8,128)(2,1)} %bitcast.668), calls=%async_computation.12 | async-start | bytes 1572864 | tf_op jit(solution)/shard_map/all_to_all | solution.py:189
  434.0 21.0 %all-to-all-start.7 = ((bf16[4,2,64,768]{3,2,1,0:T(8,128)(2,1)}), bf16[4,2,64,768]{3,2,1,0:T(8,128)(2,1)}, u32[]{:S(2)}, u32[]{:S(2)}) async-start(bf16[4,2,64,768]{3,2,1,0:T(8,128)(2,1)} %copy.229), calls=%async_computation.13 | async-start | bytes 1572864 | tf_op jit(solution)/shard_map/all_to_all | solution.py:205
  455.0 21.7 %all-to-all-start.5 = ((bf16[4,2,64,768]{3,2,1,0:T(8,128)(2,1)}), bf16[4,2,64,768]{3,2,1,0:T(8,128)(2,1)}, u32[]{:S(2)}, u32[]{:S(2)}) async-start(bf16[4,2,64,768]{3,2,1,0:T(8,128)(2,1)} %copy.225), calls=%async_computation.10 | async-start | bytes 1572864 | tf_op jit(solution)/shard_map/all_to_all | solution.py:117
  459.2 62.6 %reduce-scatter.25.cloned.1.call-start = ((), (), s32[]{:S(2)}) async-start(), calls=%async_computation.30 | async-start | bytes 491520 | tf_op jit(solution)/shard_map/reduce_scatter | solution.py:52
  459.6 36.4 %copy-start.102 = (f32[1,256,2,8]{1,3,2,0:T(8,128)}, f32[1,256,2,8]{1,3,2,0:T(8,128)S(1)}, u32[]{:S(2)}) copy-start(f32[1,256,2,8]{1,3,2,0:T(8,128)S(1)} %fusion.338) | copy-start | bytes 49156
  496.0 25.9 %copy-start.43 = (bf16[1,64,768]{2,1,0:T(8,128)(2,1)S(1)}, bf16[1,64,768]{2,1,0:T(8,128)(2,1)}, u32[]{:S(2)}) copy-start(bf16[1,64,768]{2,1,0:T(8,128)(2,1)} %reduce-scatter.21.cloned.1.call-done) | copy-start | bytes 294916
  498.5 51.5 %copy-start.51 = (f32[2,1,64,768]{3,2,1,0:T(8,128)S(1)}, f32[2,1,64,768]{3,2,1,0:T(8,128)}, u32[]{:S(2)}) copy-start(f32[2,1,64,768]{3,2,1,0:T(8,128)} %param.12) | copy-start | bytes 1179652
  498.5 51.5 %reduce-scatter.23.cloned.1.call-start = ((), (), s32[]{:S(2)}) async-start(), calls=%async_computation.29 | async-start | bytes 491520 | tf_op jit(solution)/shard_map/reduce_scatter | solution.py:52
  499.2 102.2 %reduce-scatter.27.cloned.1.call-start = ((), (), s32[]{:S(2)}) async-start(), calls=%async_computation.31 | async-start | bytes 491520 | tf_op jit(solution)/shard_map/reduce_scatter | solution.py:52
  574.0 27.5 %copy-start.61 = (f32[768]{0:T(1024)S(1)}, f32[768]{0:T(1024)}, u32[]{:S(2)}) copy-start(f32[768]{0:T(1024)} %copy-done.59) | copy-start | bytes 9220
  574.0 27.5 %copy-start.131 = (f32[64]{0:T(128)S(1)}, f32[64]{0:T(128)}, u32[]{:S(2)}) copy-start(f32[64]{0:T(128)} %copy-done.130) | copy-start | bytes 772
  574.0 27.5 %copy-start.146 = (f32[64]{0:T(128)S(1)}, f32[64]{0:T(128)}, u32[]{:S(2)}) copy-start(f32[64]{0:T(128)} %copy-done.145) | copy-start | bytes 772
  574.0 32.0 %copy-start.134 = (f32[1,256,2]{1,2,0:T(2,128)S(1)}, f32[1,256,2]{1,2,0:T(2,128)}, u32[]{:S(2)}) copy-start(f32[1,256,2]{1,2,0:T(2,128)} %get-tuple-element.81) | copy-start | bytes 6148
  604.7 3.4 collective-permute-start.2
  655.3 23.3 %all-to-all-start.9 = ((bf16[4,2,64,768]{3,2,1,0:T(8,128)(2,1)}), bf16[4,2,64,768]{3,2,1,0:T(8,128)(2,1)}, u32[]{:S(2)}, u32[]{:S(2)}) async-start(bf16[4,2,64,768]{3,2,1,0:T(8,128)(2,1)} %copy.239), calls=%async_computation.17 | async-start | bytes 1572864 | tf_op jit(solution)/shard_map/all_to_all | solution.py:205
  659.5 58.9 %reduce-scatter.29.cloned.1.call-start = ((), (), s32[]{:S(2)}) async-start(), calls=%async_computation.32 | async-start | bytes 491520 | tf_op jit(solution)/shard_map/reduce_scatter | solution.py:52
  665.6 27.2 %copy-start.124 = (f32[1,256,1]{1,2,0:T(1,128)}, f32[1,256,1]{1,2,0:T(1,128)S(1)}, u32[]{:S(2)}) copy-start(f32[1,256,1]{1,2,0:T(1,128)S(1)} %fusion.383) | copy-start | bytes 3076
  692.8 25.5 %copy-start.34 = (bf16[1,64,768]{2,1,0:T(8,128)(2,1)S(1)}, bf16[1,64,768]{2,1,0:T(8,128)(2,1)}, u32[]{:S(2)}) copy-start(bf16[1,64,768]{2,1,0:T(8,128)(2,1)} %reduce-scatter.17.cloned.1.call-done) | copy-start | bytes 294916
  692.8 25.5 %copy-start.129 = (f32[64]{0:T(128)S(1)}, f32[64]{0:T(128)}, u32[]{:S(2)}) copy-start(f32[64]{0:T(128)} %copy-done.128) | copy-start | bytes 772
  692.8 25.5 %copy-start.144 = (f32[64]{0:T(128)S(1)}, f32[64]{0:T(128)}, u32[]{:S(2)}) copy-start(f32[64]{0:T(128)} %copy-done.143) | copy-start | bytes 772
  692.8 27.1 %copy-start.52 = (f32[2,1,64,768]{3,2,1,0:T(8,128)S(1)}, f32[2,1,64,768]{3,2,1,0:T(8,128)}, u32[]{:S(2)}) copy-start(f32[2,1,64,768]{3,2,1,0:T(8,128)} %param.12) | copy-start | bytes 1179652
  692.9 27.1 %copy-start.67 = (bf16[1,64,768]{2,1,0:T(8,128)(2,1)S(1)}, bf16[1,64,768]{2,1,0:T(8,128)(2,1)}, u32[]{:S(2)}) copy-start(bf16[1,64,768]{2,1,0:T(8,128)(2,1)} %copy-done.66) | copy-start | bytes 294916
  695.4 74.2 %reduce-scatter.31.cloned.1.call-start = ((), (), s32[]{:S(2)}) async-start(), calls=%async_computation.33 | async-start | bytes 491520 | tf_op jit(solution)/shard_map/reduce_scatter | solution.py:52
  742.0 27.6 %copy-start.141 = (f32[64]{0:T(128)S(1)}, f32[64]{0:T(128)}, u32[]{:S(2)}) copy-start(f32[64]{0:T(128)} %copy-done.140) | copy-start | bytes 772
  772.3 3.5 collective-permute-start.3
  775.8 114.7 %copy-start.49 = (bf16[1,64,768]{2,1,0:T(8,128)(2,1)}, bf16[1,64,768]{2,1,0:T(8,128)(2,1)S(1)}, u32[]{:S(2)}) copy-start(bf16[1,64,768]{2,1,0:T(8,128)(2,1)S(1)} %collective-permute-done.3) | copy-start | bytes 294916
  797.8 24.5 %all-to-all-start.10 = ((bf16[4,2,64,768]{3,2,1,0:T(8,128)(2,1)}), bf16[4,2,64,768]{3,2,1,0:T(8,128)(2,1)}, u32[]{:S(2)}, u32[]{:S(2)}) async-start(bf16[4,2,64,768]{3,2,1,0:T(8,128)(2,1)} %bitcast.667), calls=%async_computation.20 | async-start | bytes 1572864 | tf_op jit(solution)/shard_map/all_to_all | solution.py:189
  827.0 23.9 %all-to-all-start.11 = ((bf16[4,2,64,768]{3,2,1,0:T(8,128)(2,1)}), bf16[4,2,64,768]{3,2,1,0:T(8,128)(2,1)}, u32[]{:S(2)}, u32[]{:S(2)}) async-start(bf16[4,2,64,768]{3,2,1,0:T(8,128)(2,1)} %copy.249), calls=%async_computation.21 | async-start | bytes 1572864 | tf_op jit(solution)/shard_map/all_to_all | solution.py:205
  831.2 58.1 %reduce-scatter.33.cloned.1.call-start = ((), (), s32[]{:S(2)}) async-start(), calls=%async_computation.34 | async-start | bytes 491520 | tf_op jit(solution)/shard_map/reduce_scatter | solution.py:52
  866.4 73.5 %reduce-scatter.35.cloned.1.call-start = ((), (), s32[]{:S(2)}) async-start(), calls=%async_computation.35 | async-start | bytes 491520 | tf_op jit(solution)/shard_map/reduce_scatter | solution.py:52
  915.0 110.0 %all-reduce.10.cloned.1.call-start = ((), (), s32[]{:S(2)}) async-start(), calls=%async_computation.36 | async-start | bytes 2359296 | tf_op jit(solution)/shard_map/psum | solution.py:344
  926.6 95.5 %copy-start.50 = (bf16[1,64,768]{2,1,0:T(8,128)(2,1)S(1)}, bf16[1,64,768]{2,1,0:T(8,128)(2,1)}, u32[]{:S(2)}) copy-start(bf16[1,64,768]{2,1,0:T(8,128)(2,1)} %copy-done.49) | copy-start | bytes 294916
  (115 other events, 750.9 us)
Sparse Core Ops, SparseCore 0:
  28.5 25.0 reduce-scatter.12
  138.1 22.8 reduce-scatter.14
  181.8 24.7 reduce-scatter.16
  291.7 22.8 reduce-scatter.18
  332.7 24.7 reduce-scatter.20
  498.6 23.2 reduce-scatter.24
  525.2 24.6 reduce-scatter.22
  576.7 24.7 reduce-scatter.26
  695.5 22.8 reduce-scatter.28
  744.8 24.7 reduce-scatter.30
  866.4 22.8 reduce-scatter.32
  915.1 24.7 reduce-scatter.34
  942.9 57.7 all-reduce.9
where the time goes:
time: 1050 us; the launch traced here: 1040 us
  waiting for transfers between devices  348 us (33%)
  blocking collectives  264 us (25%)
  local copies, waits for them, and re-layouts  125 us (12%)
  matrix products  124 us (12%)
  other arithmetic  112 us (11%)
  starting transfers between devices  46.3 us (4%)
  between operations  16.3 us (2%)
    reduce_scatter x12, waiting for transfers between devices, sum_rows(): lax.psum_scatter(block_terms.astype(jnp.bfloat16), 'tensor', scatter_dime...  251 us
    all_gather x12, blocking collectives, gather_rows(): return lax.all_gather(block_part, 'tensor', axis=1, tiled=True)  118 us
    psum x1, blocking collectives, per_device(): lax.psum((gain_sum, shift_sum, router_sum), ('tensor', 'expert'))  79.7 us
    all_to_all x2, blocking collectives, forward(): lax.all_to_all(sending, 'expert', split_axis=0, concat_axis=0, tiled=True)  43.9 us
    all_to_all x3, waiting for transfers between devices, forward(): lax.all_to_all(partial_out.astype(jnp.bfloat16), 'expert', split_axis=0,...  40.3 us
    all_to_all x3, waiting for transfers between devices, backward(): lax.all_to_all(input_part.astype(jnp.bfloat16), 'expert', split_axis=0, c...  33.5 us
    gather x6, local copies, waits for them, and re-layouts, backward(): routed = jnp.sum(table_in[cell_index], axis=2)  22.9 us
    gather x6, local copies, waits for them, and re-layouts, forward(): table_out[cell_index]  22.9 us
  transfers between devices with their start and end apart: 26, of which 23 were waited for; matrix products, arithmetic and copies ran while one was open for 11% of the time, Pallas kernels for 0%

commit v1 on v0

--- a/solution.py
+++ b/solution.py
@@ -8,6 +8,11 @@
 half_root = 0.7071067811865476
 tau_root = 0.3989422804014327
 highest = lax.Precision.HIGHEST
+
+
+def update_wires_in(base_x, mesh_ax, across):
+    taken_in = lax.psum(lax.psum(base_x, axis_name=mesh_ax), axis_name=across)
+    return taken_in
 
 
 def shifted(block, axis, distance):
@@ -344,8 +349,8 @@
         lax.psum(qkv_sum.astype(jnp.bfloat16), "expert").astype(jnp.float32),
         lax.psum(attn_sum.astype(jnp.bfloat16), "expert").astype(jnp.float32),
     )
-    gain_total, shift_total, router_total = lax.psum(
-        (gain_sum, shift_sum, router_sum), ("tensor", "expert")
+    gain_total, shift_total, router_total = update_wires_in(
+        (gain_sum, shift_sum, router_sum), "expert", "tensor"
     )
     return (
         section_out,

time: 1050 us -> 1020 us (0.971)
  blocking collectives: 264 us -> 223 us
  waiting for transfers between devices: 348 us -> 364 us
    psum x1 -> x2, blocking collectives: 79.7 us -> 38 us  [update_wires_in(): taken_in = lax.psum(lax.psum(base_x, axis_name=mesh_ax), axis_name=across)]
    psum x1, waiting for transfers between devices: 0.01 us -> 16.5 us  [per_device(): lax.psum(qkv_sum.astype(jnp.bfloat16), 'expert').astype(jnp.float32)]
  transfers between devices with their start and end apart: 26 -> 26, of which waited for: 23 -> 24; matrix products, arithmetic and copies ran while one was open for 11% -> 11% of each run, Pallas kernels for 0% -> 0%
where the time goes in v1:
time: 1020 us; the launch traced here: 1010 us
  waiting for transfers between devices  364 us (36%)
  blocking collectives  223 us (22%)
  local copies, waits for them, and re-layouts  125 us (12%)
  matrix products  124 us (12%)
  other arithmetic  112 us (11%)
  starting transfers between devices  46.3 us (5%)
  between operations  16.3 us (2%)
    reduce_scatter x12, waiting for transfers between devices, sum_rows(): lax.psum_scatter(block_terms.astype(jnp.bfloat16), 'tensor', scatter_dime...  251 us
    all_gather x12, blocking collectives, gather_rows(): return lax.all_gather(block_part, 'tensor', axis=1, tiled=True)  118 us
    all_to_all x2, blocking collectives, forward(): lax.all_to_all(sending, 'expert', split_axis=0, concat_axis=0, tiled=True)  43.9 us
    all_to_all x3, waiting for transfers between devices, forward(): lax.all_to_all(partial_out.astype(jnp.bfloat16), 'expert', split_axis=0,...  40.3 us
    psum x2, blocking collectives, update_wires_in(): taken_in = lax.psum(lax.psum(base_x, axis_name=mesh_ax), axis_name=across)  38 us
    all_to_all x3, waiting for transfers between devices, backward(): lax.all_to_all(input_part.astype(jnp.bfloat16), 'expert', split_axis=0, c...  33.5 us
    gather x6, local copies, waits for them, and re-layouts, backward(): routed = jnp.sum(table_in[cell_index], axis=2)  22.9 us
    gather x6, local copies, waits for them, and re-layouts, forward(): table_out[cell_index]  22.9 us
  transfers between devices with their start and end apart: 26, of which 24 were waited for; matrix products, arithmetic and copies ran while one was open for 11% of the time, Pallas kernels for 0%

profile of v1, /device:TPU:0, one launch (start us, length us, event | category | flops | bytes accessed | tf_op | source)
XLA Modules:
  0.0 1010.4 jit_solution(9070218246268693195)
XLA Ops:
  11.4 11.0 %all_gather.36 = bf16[1,256,768]{2,1,0:T(8,128)(2,1)S(1)} all-gather(bf16[1,64,768]{2,1,0:T(8,128)(2,1)S(1)} %fusion.264), channel_id=1, replica_groups=mesh['section'=2,'tensor'=4,'expert'=4] {'tensor'}, dimensions={1}, use_global_device_ids=true | all-gather | bytes 491520 | tf_op jit(solution)/shard_map/all_gather | solution.py:53
  29.3 24.2 %reduce-scatter.13.cloned.1.call-done = bf16[1,64,768]{2,1,0:T(8,128)(2,1)} async-done(((bf16[1,256,768]{2,1,0:T(8,128)(2,1)}), bf16[1,64,768]{2,1,0:T(8,128)(2,1)}) %reduce-scatter.13.cloned.1.call-update) | async-done | bytes 98320 | tf_op jit(solution)/shard_map/reduce_scatter | solution.py:57
  56.7 9.9 all_gather.37
  76.3 21.7 %all_to_all.60 = bf16[4,2,64,768]{3,2,1,0:T(8,128)(2,1)S(1)} all-to-all(bf16[4,2,64,768]{3,2,1,0:T(8,128)(2,1)S(1)} %bitcast.666), channel_id=1, replica_groups=mesh['section'=2,'tensor'=4,'expert'=4] {'expert'}, dimensions={0} | all-to-all | bytes 1572864 | tf_op jit(solution)/shard_map/all_to_all | solution.py:117
  101.1 4.2 all-to-all-start.1
  107.6 16.3 %all-to-all-done.1 = bf16[4,2,64,768]{3,2,1,0:T(8,128)(2,1)} async-done(((bf16[4,2,64,768]{3,2,1,0:T(8,128)(2,1)}), bf16[4,2,64,768]{3,2,1,0:T(8,128)(2,1)}, u32[]{:S(2)}, u32[]{:S(2)}) %all-to-all-start.1) | async-done | bytes 786464 | tf_op jit(solution)/shard_map/all_to_all | solution.py:122
  126.2 4.6 gather_fusion
  138.1 22.9 %reduce-scatter.15.cloned.1.call-done = bf16[1,64,768]{2,1,0:T(8,128)(2,1)} async-done(((bf16[1,256,768]{2,1,0:T(8,128)(2,1)}), bf16[1,64,768]{2,1,0:T(8,128)(2,1)}) %reduce-scatter.15.cloned.1.call-update) | async-done | bytes 98320 | tf_op jit(solution)/shard_map/reduce_scatter | solution.py:57
  164.7 9.5 all_gather.38
  184.1 22.5 %reduce-scatter.17.cloned.1.call-done = bf16[1,64,768]{2,1,0:T(8,128)(2,1)} async-done(((bf16[1,256,768]{2,1,0:T(8,128)(2,1)}), bf16[1,64,768]{2,1,0:T(8,128)(2,1)}) %reduce-scatter.17.cloned.1.call-update) | async-done | bytes 98320 | tf_op jit(solution)/shard_map/reduce_scatter | solution.py:57
  209.8 9.9 all_gather.39
  229.4 22.2 %all_to_all.61 = bf16[4,2,64,768]{3,2,1,0:T(8,128)(2,1)S(1)} all-to-all(bf16[4,2,64,768]{3,2,1,0:T(8,128)(2,1)S(1)} %bitcast.667), channel_id=1, replica_groups=mesh['section'=2,'tensor'=4,'expert'=4] {'expert'}, dimensions={0} | all-to-all | bytes 1572864 | tf_op jit(solution)/shard_map/all_to_all | solution.py:117
  254.6 4.2 all-to-all-start.3
  260.2 17.1 %all-to-all-done.3 = bf16[4,2,64,768]{3,2,1,0:T(8,128)(2,1)} async-done(((bf16[4,2,64,768]{3,2,1,0:T(8,128)(2,1)}), bf16[4,2,64,768]{3,2,1,0:T(8,128)(2,1)}, u32[]{:S(2)}, u32[]{:S(2)}) %all-to-all-start.3) | async-done | bytes 786464 | tf_op jit(solution)/shard_map/all_to_all | solution.py:122
  279.7 4.6 gather_fusion.1
  291.6 22.9 %reduce-scatter.19.cloned.1.call-done = bf16[1,64,768]{2,1,0:T(8,128)(2,1)} async-done(((bf16[1,256,768]{2,1,0:T(8,128)(2,1)}), bf16[1,64,768]{2,1,0:T(8,128)(2,1)}) %reduce-scatter.19.cloned.1.call-update) | async-done | bytes 98320 | tf_op jit(solution)/shard_map/reduce_scatter | solution.py:57
  318.2 9.5 all_gather.40
  332.9 24.6 %reduce-scatter.21.cloned.1.call-done = bf16[1,64,768]{2,1,0:T(8,128)(2,1)} async-done(((bf16[1,256,768]{2,1,0:T(8,128)(2,1)}), bf16[1,64,768]{2,1,0:T(8,128)(2,1)}) %reduce-scatter.21.cloned.1.call-update) | async-done | bytes 98320 | tf_op jit(solution)/shard_map/reduce_scatter | solution.py:57
  360.7 10.1 all_gather.41
  381.2 4.6 all-to-all-start.4
  386.8 8.1 all_gather.42
  401.3 4.5 scatter_custom_fusion.3
  408.0 5.1 all-to-all-start.6
  416.9 12.5 %all-to-all-done.6 = bf16[4,2,64,768]{3,2,1,0:T(8,128)(2,1)} async-done(((bf16[4,2,64,768]{3,2,1,0:T(8,128)(2,1)}), bf16[4,2,64,768]{3,2,1,0:T(8,128)(2,1)}, u32[]{:S(2)}, u32[]{:S(2)}) %all-to-all-start.6) | async-done | bytes 786464 | tf_op jit(solution)/shard_map/all_to_all | solution.py:194
  434.0 4.4 all-to-all-start.7
  441.6 13.4 %all-to-all-done.7 = bf16[4,2,64,768]{3,2,1,0:T(8,128)(2,1)} async-done(((bf16[4,2,64,768]{3,2,1,0:T(8,128)(2,1)}), bf16[4,2,64,768]{3,2,1,0:T(8,128)(2,1)}, u32[]{:S(2)}, u32[]{:S(2)}) %all-to-all-start.7) | async-done | bytes 786464 | tf_op jit(solution)/shard_map/all_to_all | solution.py:210
  455.0 4.2 all-to-all-start.5
  462.1 4.6 gather_fusion.3
  469.8 7.0 all-to-all-done.5
  479.1 4.6 gather_fusion.2
  486.8 5.0 multiply_reduce_fusion.2
  501.8 20.1 %reduce-scatter.25.cloned.1.call-done = bf16[1,64,768]{2,1,0:T(8,128)(2,1)} async-done(((bf16[1,256,768]{2,1,0:T(8,128)(2,1)}), bf16[1,64,768]{2,1,0:T(8,128)(2,1)}) %reduce-scatter.25.cloned.1.call-update) | async-done | bytes 98320 | tf_op jit(solution)/shard_map/reduce_scatter | solution.py:57
  524.0 26.0 %reduce-scatter.23.cloned.1.call-done = bf16[1,64,768]{2,1,0:T(8,128)(2,1)} async-done(((bf16[1,256,768]{2,1,0:T(8,128)(2,1)}), bf16[1,64,768]{2,1,0:T(8,128)(2,1)}) %reduce-scatter.23.cloned.1.call-update) | async-done | bytes 98320 | tf_op jit(solution)/shard_map/reduce_scatter | solution.py:57
  551.6 10.3 %all_gather.43 = bf16[1,256,768]{2,1,0:T(8,128)(2,1)S(1)} all-gather(bf16[1,64,768]{2,1,0:T(8,128)(2,1)S(1)} %get-tuple-element.49), channel_id=1, replica_groups=mesh['section'=2,'tensor'=4,'expert'=4] {'tensor'}, dimensions={1}, use_global_device_ids=true | all-gather | bytes 491520 | tf_op jit(solution)/shard_map/all_gather | solution.py:53
  576.6 24.9 %reduce-scatter.27.cloned.1.call-done = bf16[1,64,768]{2,1,0:T(8,128)(2,1)} async-done(((bf16[1,256,768]{2,1,0:T(8,128)(2,1)}), bf16[1,64,768]{2,1,0:T(8,128)(2,1)}) %reduce-scatter.27.cloned.1.call-update) | async-done | bytes 98320 | tf_op jit(solution)/shard_map/reduce_scatter | solution.py:57
  608.8 9.5 all_gather.44
  623.1 4.5 scatter_custom_fusion.4
  628.7 22.8 %all_to_all.62 = bf16[4,2,64,768]{3,2,1,0:T(8,128)(2,1)S(1)} all-to-all(bf16[4,2,64,768]{3,2,1,0:T(8,128)(2,1)S(1)} %bitcast.662), channel_id=1, replica_groups=mesh['section'=2,'tensor'=4,'expert'=4] {'expert'}, dimensions={0} | all-to-all | bytes 1572864 | tf_op jit(solution)/shard_map/all_to_all | solution.py:194
  655.3 4.2 all-to-all-start.9
  665.6 12.9 %all-to-all-done.9 = bf16[4,2,64,768]{3,2,1,0:T(8,128)(2,1)} async-done(((bf16[4,2,64,768]{3,2,1,0:T(8,128)(2,1)}), bf16[4,2,64,768]{3,2,1,0:T(8,128)(2,1)}, u32[]{:S(2)}, u32[]{:S(2)}) %all-to-all-start.9) | async-done | bytes 786464 | tf_op jit(solution)/shard_map/all_to_all | solution.py:210
  681.0 4.6 gather_fusion.4
  688.6 4.2 reduce.50
  698.0 20.4 %reduce-scatter.29.cloned.1.call-done = bf16[1,64,768]{2,1,0:T(8,128)(2,1)} async-done(((bf16[1,256,768]{2,1,0:T(8,128)(2,1)}), bf16[1,64,768]{2,1,0:T(8,128)(2,1)}) %reduce-scatter.29.cloned.1.call-update) | async-done | bytes 98320 | tf_op jit(solution)/shard_map/reduce_scatter | solution.py:57
  721.7 9.9 all_gather.45
  745.8 23.7 %reduce-scatter.31.cloned.1.call-done = bf16[1,64,768]{2,1,0:T(8,128)(2,1)} async-done(((bf16[1,256,768]{2,1,0:T(8,128)(2,1)}), bf16[1,64,768]{2,1,0:T(8,128)(2,1)}) %reduce-scatter.31.cloned.1.call-update) | async-done | bytes 98320 | tf_op jit(solution)/shard_map/reduce_scatter | solution.py:57
  775.9 10.5 %all_gather.46 = bf16[1,256,768]{2,1,0:T(8,128)(2,1)S(1)} all-gather(bf16[1,64,768]{2,1,0:T(8,128)(2,1)S(1)} %fusion.297), channel_id=1, replica_groups=mesh['section'=2,'tensor'=4,'expert'=4] {'tensor'}, dimensions={1}, use_global_device_ids=true | all-gather | bytes 491520 | tf_op jit(solution)/shard_map/all_gather | solution.py:53
  791.3 4.5 scatter_custom_fusion.5
  797.8 4.6 all-to-all-start.10
  802.4 4.4 fusion.162
  806.9 4.2 fusion.178
  816.0 6.4 all-to-all-done.10
  827.0 4.2 all-to-all-start.11
  836.4 4.7 fusion.175
  843.7 7.2 all-to-all-done.11
  853.3 4.6 gather_fusion.5
  866.4 4.5 fusion.160
  877.0 12.3 %reduce-scatter.33.cloned.1.call-done = bf16[1,64,768]{2,1,0:T(8,128)(2,1)} async-done(((bf16[1,256,768]{2,1,0:T(8,128)(2,1)}), bf16[1,64,768]{2,1,0:T(8,128)(2,1)}) %reduce-scatter.33.cloned.1.call-update) | async-done | bytes 98320 | tf_op jit(solution)/shard_map/reduce_scatter | solution.py:57
  891.5 9.9 all_gather.47
  915.4 7.7 fusion.6
  926.6 7.1 fusion.7
  933.7 6.2 reduce-scatter.35.cloned.1.call-done
  942.5 21.6 %all-reduce.6 = (f32[2,768]{1,0:T(2,128)S(1)}, f32[2,768]{1,0:T(2,128)S(1)}, f32[768,8]{0,1:T(8,128)S(1)}) all-reduce(f32[2,768]{1,0:T(2,128)S(1)} %fusion.355, f32[2,768]{1,0:T(2,128)S(1)} %fusion.356, f32[768,8]{0,1:T(8,128)} %convolution_add_fusion.5), channel_id=1, replica_groups=mesh['section'=2,'tensor'=4,'expert'=4] {'expert'}, use_global_device_ids=true, to_apply=%region_66.67 | all-reduce | flops 9216 | bytes 73728 | tf_op jit(solution)/shard_map/psum | solution.py:14
  964.1 16.4 %all-reduce.7 = (f32[1,2,768]{2,1,0:T(2,128)}, f32[1,2,768]{2,1,0:T(2,128)}, f32[1,768,8]{1,2,0:T(8,128)}) all-reduce(f32[1,2,768]{2,1,0:T(2,128)S(1)} %bitcast.736, f32[1,2,768]{2,1,0:T(2,128)S(1)} %bitcast.737, f32[1,768,8]{1,2,0:T(8,128)S(1)} %bitcast.723), channel_id=1, replica_groups=mesh['section'=2,'tensor'=4,'expert'=4] {'tensor'}, use_global_device_ids=true, to_apply=%region_67.68 | all-reduce | flops 9216 | bytes 73728 | tf_op jit(solution)/shard_map/psum | solution.py:14
  983.4 16.5 %all-reduce.11.cloned.1.call-done = (bf16[1,3,768,3,64]{2,4,3,1,0:T(8,128)(2,1)}, bf16[1,3,64,768]{3,2,1,0:T(8,128)(2,1)}) async-done(((bf16[1,3,768,3,64]{2,4,3,1,0:T(8,128)(2,1)}, bf16[1,3,64,768]{3,2,1,0:T(8,128)(2,1)}), (bf16[1,3,768,3,64]{2,4,3,1,0:T(8,128)(2,1)}, bf16[1,3,64,768]{3,2,1,0:T(8,128)(2,1)})) %all-reduce.11.cloned.1.call-update) | async-done | bytes 1179664 | tf_op jit(solution)/shard_map/psum | solution.py:349
  (579 shorter events, 288.6 us)
Async XLA Ops:
  7.2 91.9 %copy-start = (bf16[1,2,768,768]{3,2,1,0:T(8,128)(2,1)S(1)}, bf16[1,2,768,768]{3,2,1,0:T(8,128)(2,1)}, u32[]{:S(2)}) copy-start(bf16[1,2,768,768]{3,2,1,0:T(8,128)(2,1)} %param.19) | copy-start | bytes 7077892
  7.2 46.3 %reduce-scatter.13.cloned.1.call-start = ((), (), s32[]{:S(2)}) async-start(), calls=%async_computation.24 | async-start | bytes 491520 | tf_op jit(solution)/shard_map/reduce_scatter | solution.py:57
  10.4 45.3 %copy-start.95 = (f32[768]{0:T(1024)}, f32[768]{0:T(1024)S(1)}, u32[]{:S(2)}) copy-start(f32[768]{0:T(1024)S(1)} %get-tuple-element.38) | copy-start | bytes 9220
  10.4 154.2 %copy-start.59 = (f32[768]{0:T(1024)}, f32[768]{0:T(1024)S(1)}, u32[]{:S(2)}) copy-start(f32[768]{0:T(1024)S(1)} %get-tuple-element.89) | copy-start | bytes 9220
  10.4 154.2 %copy-start.100 = (f32[768]{0:T(1024)}, f32[768]{0:T(1024)S(1)}, u32[]{:S(2)}) copy-start(f32[768]{0:T(1024)S(1)} %get-tuple-element.37) | copy-start | bytes 9220
  24.3 29.2 %copy-start.12 = (bf16[2,1,64,768]{3,2,1,0:T(8,128)(2,1)S(1)}, bf16[2,1,64,768]{3,2,1,0:T(8,128)(2,1)}, u32[]{:S(2)}) copy-start(bf16[2,1,64,768]{3,2,1,0:T(8,128)(2,1)} %param.11) | copy-start | bytes 589828
  27.3 40.6 %copy-start.71 = (bf16[3,64,256]{2,1,0:T(8,128)(2,1)}, bf16[3,64,256]{2,1,0:T(8,128)(2,1)S(1)}, u32[]{:S(2)}) copy-start(bf16[3,64,256]{2,1,0:T(8,128)(2,1)S(1)} %convolution_convert_fusion.14) | copy-start | bytes 294916
  29.3 41.6 %copy-start.149 = (s32[512,1]{0,1:T(1,128)}, s32[512,1]{0,1:T(1,128)S(1)}, u32[]{:S(2)}) copy-start(s32[512,1]{0,1:T(1,128)S(1)} %compare_select_fusion.2) | copy-start | bytes 6148
  66.6 39.9 %copy-start.17 = (bf16[1,256,768]{2,1,0:T(8,128)(2,1)}, bf16[1,256,768]{2,1,0:T(8,128)(2,1)S(1)}, u32[]{:S(2)}) copy-start(bf16[1,256,768]{2,1,0:T(8,128)(2,1)S(1)} %all_gather.37) | copy-start | bytes 1179652
  101.1 22.7 %all-to-all-start.1 = ((bf16[4,2,64,768]{3,2,1,0:T(8,128)(2,1)}), bf16[4,2,64,768]{3,2,1,0:T(8,128)(2,1)}, u32[]{:S(2)}, u32[]{:S(2)}) async-start(bf16[4,2,64,768]{3,2,1,0:T(8,128)(2,1)} %copy.213), calls=%async_computation.2 | async-start | bytes 1572864 | tf_op jit(solution)/shard_map/all_to_all | solution.py:122
  105.3 55.7 %reduce-scatter.15.cloned.1.call-start = ((), (), s32[]{:S(2)}) async-start(), calls=%async_computation.25 | async-start | bytes 491520 | tf_op jit(solution)/shard_map/reduce_scatter | solution.py:57
  106.5 24.3 %copy-start.105 = (s32[256,2]{0,1:T(2,128)}, s32[256,2]{0,1:T(2,128)S(1)}, u32[]{:S(2)}) copy-start(s32[256,2]{0,1:T(2,128)S(1)} %get-tuple-element.80) | copy-start | bytes 6148
  133.8 27.2 %copy-start.23 = (bf16[1,64,768]{2,1,0:T(8,128)(2,1)S(1)}, bf16[1,64,768]{2,1,0:T(8,128)(2,1)}, u32[]{:S(2)}) copy-start(bf16[1,64,768]{2,1,0:T(8,128)(2,1)} %reduce-scatter.13.cloned.1.call-done) | copy-start | bytes 294916
  138.0 68.6 %reduce-scatter.17.cloned.1.call-start = ((), (), s32[]{:S(2)}) async-start(), calls=%async_computation.26 | async-start | bytes 491520 | tf_op jit(solution)/shard_map/reduce_scatter | solution.py:57
  162.0 2.2 collective-permute-start
  177.6 31.1 %copy-start.41 = (f32[3,256,256]{1,2,0:T(8,128)}, f32[3,256,256]{1,2,0:T(8,128)S(1)}, u32[]{:S(2)}) copy-start(f32[3,256,256]{1,2,0:T(8,128)S(1)} %convolution_multiply_fusion.1) | copy-start | bytes 2359300
  177.6 31.1 %copy-start.96 = (f32[768]{0:T(1024)S(1)}, f32[768]{0:T(1024)}, u32[]{:S(2)}) copy-start(f32[768]{0:T(1024)} %copy-done.95) | copy-start | bytes 9220
  219.7 39.5 %copy-start.19 = (bf16[1,256,768]{2,1,0:T(8,128)(2,1)}, bf16[1,256,768]{2,1,0:T(8,128)(2,1)S(1)}, u32[]{:S(2)}) copy-start(bf16[1,256,768]{2,1,0:T(8,128)(2,1)S(1)} %all_gather.39) | copy-start | bytes 1179652
  254.6 22.7 %all-to-all-start.3 = ((bf16[4,2,64,768]{3,2,1,0:T(8,128)(2,1)}), bf16[4,2,64,768]{3,2,1,0:T(8,128)(2,1)}, u32[]{:S(2)}, u32[]{:S(2)}) async-start(bf16[4,2,64,768]{3,2,1,0:T(8,128)(2,1)} %copy.219), calls=%async_computation.6 | async-start | bytes 1572864 | tf_op jit(solution)/shard_map/all_to_all | solution.py:122
  258.8 55.7 %reduce-scatter.19.cloned.1.call-start = ((), (), s32[]{:S(2)}) async-start(), calls=%async_computation.27 | async-start | bytes 491520 | tf_op jit(solution)/shard_map/reduce_scatter | solution.py:57
  259.5 24.8 %copy-start.121 = (f32[1,256,1]{1,2,0:T(1,128)}, f32[1,256,1]{1,2,0:T(1,128)S(1)}, u32[]{:S(2)}) copy-start(f32[1,256,1]{1,2,0:T(1,128)S(1)} %get-tuple-element.56) | copy-start | bytes 3076
  287.3 27.2 %copy-start.33 = (bf16[1,64,768]{2,1,0:T(8,128)(2,1)S(1)}, bf16[1,64,768]{2,1,0:T(8,128)(2,1)}, u32[]{:S(2)}) copy-start(bf16[1,64,768]{2,1,0:T(8,128)(2,1)} %reduce-scatter.17.cloned.1.call-done) | copy-start | bytes 294916
  287.3 30.8 %copy-start.60 = (f32[768]{0:T(1024)S(1)}, f32[768]{0:T(1024)}, u32[]{:S(2)}) copy-start(f32[768]{0:T(1024)} %copy-done.59) | copy-start | bytes 9220
  287.3 30.8 %copy-start.101 = (f32[768]{0:T(1024)S(1)}, f32[768]{0:T(1024)}, u32[]{:S(2)}) copy-start(f32[768]{0:T(1024)} %copy-done.100) | copy-start | bytes 9220
  291.5 66.0 %reduce-scatter.21.cloned.1.call-start = ((), (), s32[]{:S(2)}) async-start(), calls=%async_computation.28 | async-start | bytes 491520 | tf_op jit(solution)/shard_map/reduce_scatter | solution.py:57
  315.6 2.2 collective-permute-start.1
  329.7 29.9 %copy-start.97 = (f32[768]{0:T(1024)S(1)}, f32[768]{0:T(1024)}, u32[]{:S(2)}) copy-start(f32[768]{0:T(1024)} %copy-done.95) | copy-start | bytes 9220
  331.5 40.6 %copy-start.64 = (bf16[3,64,256]{2,1,0:T(8,128)(2,1)}, bf16[3,64,256]{2,1,0:T(8,128)(2,1)S(1)}, u32[]{:S(2)}) copy-start(bf16[3,64,256]{2,1,0:T(8,128)(2,1)S(1)} %convolution_convert_fusion.12) | copy-start | bytes 294916
  358.6 163.3 %copy-start.132 = (f32[64]{0:T(128)}, f32[64]{0:T(128)S(1)}, u32[]{:S(2)}) copy-start(f32[64]{0:T(128)S(1)} %broadcast_multiply_fusion.12) | copy-start | bytes 772
  359.7 162.2 %copy-start.147 = (f32[64]{0:T(128)}, f32[64]{0:T(128)S(1)}, u32[]{:S(2)}) copy-start(f32[64]{0:T(128)S(1)} %add_rsqrt_fusion) | copy-start | bytes 772
  370.8 29.9 %copy-start.20 = (bf16[1,256,768]{2,1,0:T(8,128)(2,1)}, bf16[1,256,768]{2,1,0:T(8,128)(2,1)S(1)}, u32[]{:S(2)}) copy-start(bf16[1,256,768]{2,1,0:T(8,128)(2,1)S(1)} %all_gather.41) | copy-start | bytes 1179652
  381.2 26.7 %all-to-all-start.4 = ((bf16[4,2,64,768]{3,2,1,0:T(8,128)(2,1)}), bf16[4,2,64,768]{3,2,1,0:T(8,128)(2,1)}, u32[]{:S(2)}, u32[]{:S(2)}) async-start(bf16[4,2,64,768]{3,2,1,0:T(8,128)(2,1)} %bitcast.663), calls=%async_computation.9 | async-start | bytes 1572864 | tf_op jit(solution)/shard_map/all_to_all | solution.py:117
  408.0 21.4 %all-to-all-start.6 = ((bf16[4,2,64,768]{3,2,1,0:T(8,128)(2,1)}), bf16[4,2,64,768]{3,2,1,0:T(8,128)(2,1)}, u32[]{:S(2)}, u32[]{:S(2)}) async-start(bf16[4,2,64,768]{3,2,1,0:T(8,128)(2,1)} %bitcast.665), calls=%async_computation.12 | async-start | bytes 1572864 | tf_op jit(solution)/shard_map/all_to_all | solution.py:194
  434.0 21.0 %all-to-all-start.7 = ((bf16[4,2,64,768]{3,2,1,0:T(8,128)(2,1)}), bf16[4,2,64,768]{3,2,1,0:T(8,128)(2,1)}, u32[]{:S(2)}, u32[]{:S(2)}) async-start(bf16[4,2,64,768]{3,2,1,0:T(8,128)(2,1)} %copy.229), calls=%async_computation.13 | async-start | bytes 1572864 | tf_op jit(solution)/shard_map/all_to_all | solution.py:210
  455.0 21.7 %all-to-all-start.5 = ((bf16[4,2,64,768]{3,2,1,0:T(8,128)(2,1)}), bf16[4,2,64,768]{3,2,1,0:T(8,128)(2,1)}, u32[]{:S(2)}, u32[]{:S(2)}) async-start(bf16[4,2,64,768]{3,2,1,0:T(8,128)(2,1)} %copy.225), calls=%async_computation.10 | async-start | bytes 1572864 | tf_op jit(solution)/shard_map/all_to_all | solution.py:122
  459.2 62.6 %reduce-scatter.25.cloned.1.call-start = ((), (), s32[]{:S(2)}) async-start(), calls=%async_computation.30 | async-start | bytes 491520 | tf_op jit(solution)/shard_map/reduce_scatter | solution.py:57
  459.6 36.4 %copy-start.102 = (f32[1,256,2,8]{1,3,2,0:T(8,128)}, f32[1,256,2,8]{1,3,2,0:T(8,128)S(1)}, u32[]{:S(2)}) copy-start(f32[1,256,2,8]{1,3,2,0:T(8,128)S(1)} %fusion.337) | copy-start | bytes 49156
  496.0 25.9 %copy-start.43 = (bf16[1,64,768]{2,1,0:T(8,128)(2,1)S(1)}, bf16[1,64,768]{2,1,0:T(8,128)(2,1)}, u32[]{:S(2)}) copy-start(bf16[1,64,768]{2,1,0:T(8,128)(2,1)} %reduce-scatter.21.cloned.1.call-done) | copy-start | bytes 294916
  498.5 51.5 %copy-start.51 = (f32[2,1,64,768]{3,2,1,0:T(8,128)S(1)}, f32[2,1,64,768]{3,2,1,0:T(8,128)}, u32[]{:S(2)}) copy-start(f32[2,1,64,768]{3,2,1,0:T(8,128)} %param.12) | copy-start | bytes 1179652
  498.5 51.5 %reduce-scatter.23.cloned.1.call-start = ((), (), s32[]{:S(2)}) async-start(), calls=%async_computation.29 | async-start | bytes 491520 | tf_op jit(solution)/shard_map/reduce_scatter | solution.py:57
  499.2 102.2 %reduce-scatter.27.cloned.1.call-start = ((), (), s32[]{:S(2)}) async-start(), calls=%async_computation.31 | async-start | bytes 491520 | tf_op jit(solution)/shard_map/reduce_scatter | solution.py:57
  574.0 27.5 %copy-start.61 = (f32[768]{0:T(1024)S(1)}, f32[768]{0:T(1024)}, u32[]{:S(2)}) copy-start(f32[768]{0:T(1024)} %copy-done.59) | copy-start | bytes 9220
  574.0 27.5 %copy-start.131 = (f32[64]{0:T(128)S(1)}, f32[64]{0:T(128)}, u32[]{:S(2)}) copy-start(f32[64]{0:T(128)} %copy-done.130) | copy-start | bytes 772
  574.0 27.5 %copy-start.146 = (f32[64]{0:T(128)S(1)}, f32[64]{0:T(128)}, u32[]{:S(2)}) copy-start(f32[64]{0:T(128)} %copy-done.145) | copy-start | bytes 772
  574.0 32.0 %copy-start.134 = (f32[1,256,2]{1,2,0:T(2,128)S(1)}, f32[1,256,2]{1,2,0:T(2,128)}, u32[]{:S(2)}) copy-start(f32[1,256,2]{1,2,0:T(2,128)} %get-tuple-element.84) | copy-start | bytes 6148
  604.7 3.4 collective-permute-start.2
  655.3 23.3 %all-to-all-start.9 = ((bf16[4,2,64,768]{3,2,1,0:T(8,128)(2,1)}), bf16[4,2,64,768]{3,2,1,0:T(8,128)(2,1)}, u32[]{:S(2)}, u32[]{:S(2)}) async-start(bf16[4,2,64,768]{3,2,1,0:T(8,128)(2,1)} %copy.239), calls=%async_computation.17 | async-start | bytes 1572864 | tf_op jit(solution)/shard_map/all_to_all | solution.py:210
  659.5 58.9 %reduce-scatter.29.cloned.1.call-start = ((), (), s32[]{:S(2)}) async-start(), calls=%async_computation.32 | async-start | bytes 491520 | tf_op jit(solution)/shard_map/reduce_scatter | solution.py:57
  665.6 27.2 %copy-start.124 = (f32[1,256,1]{1,2,0:T(1,128)}, f32[1,256,1]{1,2,0:T(1,128)S(1)}, u32[]{:S(2)}) copy-start(f32[1,256,1]{1,2,0:T(1,128)S(1)} %fusion.380) | copy-start | bytes 3076
  692.8 25.5 %copy-start.34 = (bf16[1,64,768]{2,1,0:T(8,128)(2,1)S(1)}, bf16[1,64,768]{2,1,0:T(8,128)(2,1)}, u32[]{:S(2)}) copy-start(bf16[1,64,768]{2,1,0:T(8,128)(2,1)} %reduce-scatter.17.cloned.1.call-done) | copy-start | bytes 294916
  692.8 25.5 %copy-start.129 = (f32[64]{0:T(128)S(1)}, f32[64]{0:T(128)}, u32[]{:S(2)}) copy-start(f32[64]{0:T(128)} %copy-done.128) | copy-start | bytes 772
  692.8 25.5 %copy-start.144 = (f32[64]{0:T(128)S(1)}, f32[64]{0:T(128)}, u32[]{:S(2)}) copy-start(f32[64]{0:T(128)} %copy-done.143) | copy-start | bytes 772
  692.8 27.1 %copy-start.52 = (f32[2,1,64,768]{3,2,1,0:T(8,128)S(1)}, f32[2,1,64,768]{3,2,1,0:T(8,128)}, u32[]{:S(2)}) copy-start(f32[2,1,64,768]{3,2,1,0:T(8,128)} %param.12) | copy-start | bytes 1179652
  692.9 27.1 %copy-start.67 = (bf16[1,64,768]{2,1,0:T(8,128)(2,1)S(1)}, bf16[1,64,768]{2,1,0:T(8,128)(2,1)}, u32[]{:S(2)}) copy-start(bf16[1,64,768]{2,1,0:T(8,128)(2,1)} %copy-done.66) | copy-start | bytes 294916
  695.4 74.2 %reduce-scatter.31.cloned.1.call-start = ((), (), s32[]{:S(2)}) async-start(), calls=%async_computation.33 | async-start | bytes 491520 | tf_op jit(solution)/shard_map/reduce_scatter | solution.py:57
  742.0 27.6 %copy-start.141 = (f32[64]{0:T(128)S(1)}, f32[64]{0:T(128)}, u32[]{:S(2)}) copy-start(f32[64]{0:T(128)} %copy-done.140) | copy-start | bytes 772
  772.3 3.5 collective-permute-start.3
  775.8 114.7 %copy-start.49 = (bf16[1,64,768]{2,1,0:T(8,128)(2,1)}, bf16[1,64,768]{2,1,0:T(8,128)(2,1)S(1)}, u32[]{:S(2)}) copy-start(bf16[1,64,768]{2,1,0:T(8,128)(2,1)S(1)} %collective-permute-done.3) | copy-start | bytes 294916
  797.8 24.5 %all-to-all-start.10 = ((bf16[4,2,64,768]{3,2,1,0:T(8,128)(2,1)}), bf16[4,2,64,768]{3,2,1,0:T(8,128)(2,1)}, u32[]{:S(2)}, u32[]{:S(2)}) async-start(bf16[4,2,64,768]{3,2,1,0:T(8,128)(2,1)} %bitcast.664), calls=%async_computation.20 | async-start | bytes 1572864 | tf_op jit(solution)/shard_map/all_to_all | solution.py:194
  827.0 23.9 %all-to-all-start.11 = ((bf16[4,2,64,768]{3,2,1,0:T(8,128)(2,1)}), bf16[4,2,64,768]{3,2,1,0:T(8,128)(2,1)}, u32[]{:S(2)}, u32[]{:S(2)}) async-start(bf16[4,2,64,768]{3,2,1,0:T(8,128)(2,1)} %copy.249), calls=%async_computation.21 | async-start | bytes 1572864 | tf_op jit(solution)/shard_map/all_to_all | solution.py:210
  831.2 58.1 %reduce-scatter.33.cloned.1.call-start = ((), (), s32[]{:S(2)}) async-start(), calls=%async_computation.34 | async-start | bytes 491520 | tf_op jit(solution)/shard_map/reduce_scatter | solution.py:57
  866.4 73.5 %reduce-scatter.35.cloned.1.call-start = ((), (), s32[]{:S(2)}) async-start(), calls=%async_computation.35 | async-start | bytes 491520 | tf_op jit(solution)/shard_map/reduce_scatter | solution.py:57
  915.0 84.8 %all-reduce.11.cloned.1.call-start = ((), (), s32[]{:S(2)}) async-start(), calls=%async_computation.36 | async-start | bytes 2359296 | tf_op jit(solution)/shard_map/psum | solution.py:349
  926.6 53.9 %copy-start.50 = (bf16[1,64,768]{2,1,0:T(8,128)(2,1)S(1)}, bf16[1,64,768]{2,1,0:T(8,128)(2,1)}, u32[]{:S(2)}) copy-start(bf16[1,64,768]{2,1,0:T(8,128)(2,1)} %copy-done.49) | copy-start | bytes 294916
  (115 other events, 750.9 us)
Sparse Core Ops, SparseCore 0:
  28.5 25.0 reduce-scatter.12
  138.1 22.8 reduce-scatter.14
  181.8 24.7 reduce-scatter.16
  291.7 22.8 reduce-scatter.18
  332.7 24.7 reduce-scatter.20
  498.6 23.2 reduce-scatter.24
  525.2 24.6 reduce-scatter.22
  576.7 24.7 reduce-scatter.26
  695.5 22.8 reduce-scatter.28
  744.8 24.7 reduce-scatter.30
  866.4 22.8 reduce-scatter.32
  915.1 24.7 reduce-scatter.34
  942.9 56.9 all-reduce.10
